TPU v7x, 32 devices: a whole 2x2x4 slice. The times are simulated.
32 devices in a mesh: row: 4 (over z), col: 4 (over x, core), layer: 2 (over y).
Axes of the slice: x: 2, y: 2, z: 4, core: 2. Of those that a mesh axis runs over, the one named last changes fastest.
Arguments:
- intersection: bfloat16 [2048, 2, 1024], P('row', 'layer', 'col'), may hold values from -6 to 6
- density: bfloat16 [2, 1024, 2, 1024], P('layer', 'row', None, 'col'), may hold values from -0.125 to 0.125
- hamiltonian: bfloat16 [2, 1024, 2, 1024], P('layer', 'row', None, 'col'), may hold values from -0.125 to 0.125
- intersection_pattern: int32 [16, 2, 8], P('row', 'layer', 'col'), may hold values 0 or 1
- density_pattern: int32 [2, 8, 2, 8], P('layer', 'row', None, 'col'), may hold values 0 or 1
- hamiltonian_pattern: int32 [2, 8, 2, 8], P('layer', 'row', None, 'col'), may hold values 0 or 1
- product_filter: int32 [16, 2, 8], P('row', 'layer', 'col'), may hold values 0 or 1
Outputs:
- gradient_term: bfloat16 [2048, 2, 1024], P('row', 'layer', 'col')
All inputs are finite; a program needn't handle non-finite values. No bound on the sum of `intersection_pattern` or of `density_pattern` or of `hamiltonian_pattern` or of `product_filter` on one device may be relied on, other than what follows from the above.
Results may differ from a plain program's by a relative error of at most 0.005.
Values may be sent and summed in bfloat16 or wider, within the bound.
No kernel may reach another device: no remote copies, remote signals or barrier semaphores. Data moves between devices by JAX's collectives and lax.ppermute only.
A program may use at most 64 MiB of HBM per device.

v0:
```python
import jax
import jax.numpy as jnp
from jax import lax
from jax.sharding import PartitionSpec as P


def mask_left(block_tile, pattern):
    row_count, _, col_count = block_tile.shape
    row_blocks = pattern.shape[0]
    col_blocks = pattern.shape[2]
    blocks = block_tile.reshape(
        row_blocks, row_count // row_blocks, col_blocks, col_count // col_blocks
    )
    blocks = blocks * pattern.reshape(row_blocks, 1, col_blocks, 1).astype(jnp.bfloat16)
    return blocks.reshape(row_count, col_count)


def mask_right(block_tile, pattern):
    _, row_count, layers, col_count = block_tile.shape
    row_blocks = pattern.shape[1]
    col_blocks = pattern.shape[3]
    blocks = block_tile.reshape(
        row_blocks, row_count // row_blocks, layers, col_blocks, col_count // col_blocks
    )
    blocks = blocks * pattern.reshape(row_blocks, 1, layers, col_blocks, 1).astype(jnp.bfloat16)
    return blocks.reshape(row_count, layers * col_count)


def multiply(left_tile, right_tile):
    whole_left = lax.all_gather(left_tile, "col", axis=1, tiled=True)
    row_count = whole_left.shape[0]
    layers = lax.axis_size("layer")
    column_span = right_tile.shape[1] // layers
    partial_value = jnp.dot(
        whole_left,
        lax.all_gather(right_tile, "row", axis=0, tiled=True),
        preferred_element_type=jnp.float32,
    )
    return lax.psum_scatter(
        partial_value.reshape(row_count, layers, column_span),
        "layer",
        scatter_dimension=1,
        tiled=True,
    )


def local(
    intersection,
    density,
    hamiltonian,
    intersection_pattern,
    density_pattern,
    hamiltonian_pattern,
    product_filter,
):
    left_factor = mask_left(intersection, intersection_pattern)
    right_factor = mask_right(density, density_pattern)
    raw_product = multiply(left_factor, right_factor)
    filtered = mask_left(raw_product.astype(jnp.bfloat16), product_filter)
    masked_ham = mask_right(hamiltonian, hamiltonian_pattern)
    return multiply(filtered, masked_ham).astype(jnp.bfloat16)


def solution(mesh):
    placed = (
        P("row", "layer", "col"),
        P("layer", "row", None, "col"),
        P("layer", "row", None, "col"),
        P("row", "layer", "col"),
        P("layer", "row", None, "col"),
        P("layer", "row", None, "col"),
        P("row", "layer", "col"),
    )
    return jax.shard_map(
        local, mesh=mesh, in_specs=placed, out_specs=P("row", "layer", "col"), check_vma=False
    )
```

profile of v0, /device:TPU:0, one launch (start us, length us, event | category | flops | bytes accessed | tf_op | source)
XLA Modules:
  0.0 161.6 jit_solution(11556054652740069047)
XLA Ops:
  6.5 0.0 all-gather.7.cloned.1.call-start
  6.5 0.7 convert_bitcast_fusion.1
  7.2 0.2 mul.47
  7.4 0.0 copy-start.1
  7.4 0.1 mul.48
  7.6 0.8 copy-done.1
  8.4 0.0 copy-start.4
  8.4 0.8 mul.49
  9.2 0.0 copy-start
  9.2 0.0 all-gather.7.cloned.1.call-update
  9.2 0.0 all-gather.5.cloned.1.call-start
  9.3 0.0 copy-done.4
  9.3 0.1 copy.8
  9.4 0.2 mul.44
  9.6 0.5 copy-done
  10.2 0.7 bitcast_multiply_fusion.1
  10.9 0.0 all-gather.5.cloned.1.call-update
  10.9 0.0 reduce-scatter.3.cloned.1.call-start
  11.0 29.0 %all-gather.7.cloned.1.call-done = bf16[1024,512]{1,0:T(8,128)(2,1)} async-done(((bf16[256,512]{1,0:T(8,128)(2,1)}), bf16[1024,512]{1,0:T(8,128)(2,1)}) %all-gather.7.cloned.1.call-update) | async-done | bytes 1048592 | tf_op jit(solution)/shard_map/all_gather | solution.py:36
  40.0 17.9 %all-gather.5.cloned.1.call-done = bf16[512,1024]{1,0:T(8,128)(2,1)} async-done(((bf16[512,256]{1,0:T(8,128)(2,1)}), bf16[512,1024]{1,0:T(8,128)(2,1)}) %all-gather.5.cloned.1.call-update) | async-done | bytes 1048592 | tf_op jit(solution)/shard_map/all_gather | solution.py:30
  57.9 3.3 %fusion = f32[512,512]{0,1:T(8,128)} fusion(bf16[512,1024]{1,0:T(8,128)(2,1)} %all-gather.5.cloned.1.call-done, bf16[1024,512]{1,0:T(8,128)(2,1)} %all-gather.7.cloned.1.call-done), kind=kOutput, calls=%fused_computation.6 | convolution fusion | flops 536870912 | bytes 3145728 | tf_op jit(solution)/shard_map/dot_general | solution.py:34
  61.2 0.0 copy-start.3
  61.2 0.0 reduce-scatter.3.cloned.1.call-update
  61.2 0.0 all-gather.11.cloned.1.call-start
  61.3 0.6 copy-done.3
  61.9 0.2 mul.53
  62.1 0.0 copy-start.2
  62.1 0.1 mul.54
  62.2 0.8 copy-done.2
  63.1 0.8 mul.55
  63.9 0.0 copy-start.5
  63.9 0.0 all-gather.11.cloned.1.call-update
  63.9 0.0 all-gather.9.cloned.1.call-start
  64.0 0.6 copy-done.5
  64.6 17.1 %reduce-scatter.3.cloned.1.call-done = f32[512,1,256]{0,2,1:T(8,128)} async-done(((f32[512,2,256]{0,2,1:T(8,128)}), f32[512,1,256]{0,2,1:T(8,128)}) %reduce-scatter.3.cloned.1.call-update) | async-done | bytes 524304 | tf_op jit(solution)/shard_map/reduce_scatter | solution.py:39
  81.7 0.1 mul.50
  81.9 1.8 %bitcast_multiply_fusion = bf16[512,256]{0,1:T(8,128)(2,1)} fusion(bf16[32,8,4,128]{3,2,1,0:T(4,128)(2,1)S(1)} %bitcast.39, f32[512,1,256]{0,2,1:T(8,128)} %reduce-scatter.3.cloned.1.call-done), kind=kLoop, calls=%fused_computation | loop fusion | flops 262144 | bytes 1048576 | tf_op jit(solution)/shard_map/mul | solution.py:14
  83.7 0.0 all-gather.9.cloned.1.call-update
  83.7 0.0 reduce-scatter.5.cloned.1.call-start
  83.7 27.4 %all-gather.11.cloned.1.call-done = bf16[1024,512]{1,0:T(8,128)(2,1)} async-done(((bf16[256,512]{1,0:T(8,128)(2,1)}), bf16[1024,512]{1,0:T(8,128)(2,1)}) %all-gather.11.cloned.1.call-update) | async-done | bytes 1048592 | tf_op jit(solution)/shard_map/all_gather | solution.py:36
  111.2 17.7 %all-gather.9.cloned.1.call-done = bf16[512,1024]{0,1:T(8,128)(2,1)} async-done(((bf16[512,256]{0,1:T(8,128)(2,1)}), bf16[512,1024]{0,1:T(8,128)(2,1)}) %all-gather.9.cloned.1.call-update) | async-done | bytes 1048592 | tf_op jit(solution)/shard_map/all_gather | solution.py:30
  128.9 2.3 %fusion.1 = f32[512,512]{0,1:T(8,128)S(1)} fusion(bf16[512,1024]{0,1:T(8,128)(2,1)} %all-gather.9.cloned.1.call-done, bf16[1024,512]{1,0:T(8,128)(2,1)} %all-gather.11.cloned.1.call-done), kind=kOutput, calls=%fused_computation.7 | convolution fusion | flops 536870912 | bytes 3145728 | tf_op jit(solution)/shard_map/dot_general | solution.py:34
  131.2 1.3 copy.9
  132.5 0.0 reduce-scatter.5.cloned.1.call-update
  132.5 20.5 %reduce-scatter.5.cloned.1.call-done = f32[512,1,256]{2,0,1:T(8,128)} async-done(((f32[512,2,256]{2,0,1:T(8,128)}), f32[512,1,256]{2,0,1:T(8,128)}) %reduce-scatter.5.cloned.1.call-update) | async-done | bytes 524304 | tf_op jit(solution)/shard_map/reduce_scatter | solution.py:39
  153.0 1.8 %convert_element_type.59 = bf16[512,1,256]{2,0,1:T(8,128)(2,1)} convert(f32[512,1,256]{2,0,1:T(8,128)} %reduce-scatter.5.cloned.1.call-done) | non-fusion elementwise | flops 131072 | bytes 786432 | tf_op jit(solution)/shard_map/convert_element_type | solution.py:61
  (5 shorter events, 0.1 us)
Async XLA Ops:
  6.5 33.5 %all-gather.7.cloned.1.call-start = ((), (), s32[]{:S(2)}) async-start(), calls=%async_computation.3 | async-start | bytes 1310720 | tf_op jit(solution)/shard_map/all_gather | solution.py:36
  7.4 1.0 copy-start.1
  8.4 0.9 copy-start.4
  9.2 0.9 copy-start
  9.2 48.7 %all-gather.5.cloned.1.call-start = ((), (), s32[]{:S(2)}) async-start(), calls=%async_computation.2 | async-start | bytes 1310720 | tf_op jit(solution)/shard_map/all_gather | solution.py:30
  10.9 70.8 %reduce-scatter.3.cloned.1.call-start = ((), (), s32[]{:S(2)}) async-start(), calls=%async_computation.4 | async-start | bytes 1572864 | tf_op jit(solution)/shard_map/reduce_scatter | solution.py:39
  61.2 0.7 copy-start.3
  61.2 49.9 %all-gather.11.cloned.1.call-start = ((), (), s32[]{:S(2)}) async-start(), calls=%async_computation.6 | async-start | bytes 1310720 | tf_op jit(solution)/shard_map/all_gather | solution.py:36
  62.1 1.0 copy-start.2
  63.9 0.7 copy-start.5
  63.9 65.0 %all-gather.9.cloned.1.call-start = ((), (), s32[]{:S(2)}) async-start(), calls=%async_computation.5 | async-start | bytes 1310720 | tf_op jit(solution)/shard_map/all_gather | solution.py:30
  83.7 69.3 %reduce-scatter.5.cloned.1.call-start = ((), (), s32[]{:S(2)}) async-start(), calls=%async_computation.7 | async-start | bytes 1572864 | tf_op jit(solution)/shard_map/reduce_scatter | solution.py:39
Sparse Core Ops, SparseCore 0:
  9.4 30.6 all-gather.6
  41.6 16.3 all-gather.4
  61.4 20.3 reduce-scatter.2
  83.2 27.9 all-gather.10
  112.7 16.2 all-gather.8
  132.7 20.3 reduce-scatter.4
where the time goes:
time: 162 us
  waiting for transfers between devices  130 us (80%)
  between operations  13.6 us (8%)
  other arithmetic  6.58 us (4%)
  local copies, waits for them, and re-layouts  5.88 us (4%)
  matrix products  5.57 us (3%)
    all_gather x2, waiting for transfers between devices, multiply(): lax.all_gather(right_tile, 'row', axis=0, tiled=True)  56.5 us
    reduce_scatter x2, waiting for transfers between devices, multiply(): lax.psum_scatter(partial_value.reshape(row_count, layers, column_span), '...  37.6 us
    all_gather x2, waiting for transfers between devices, multiply(): whole_left = lax.all_gather(left_tile, 'col', axis=1, tiled=True)  35.6 us
    dot_general x2, matrix products, multiply(): jnp.dot(whole_left, lax.all_gather(right_tile, 'row', axis=0, tiled=True)...  5.57 us
    unnamed x14, local copies, waits for them, and re-layouts  3.49 us
  transfers between devices with their start and end apart: 6, of which 6 were waited for; matrix products, arithmetic and copies ran while one was open for 3% of the time, Pallas kernels for 0%

commit v1 on v0

--- a/solution.py
+++ b/solution.py
@@ -2,6 +2,29 @@
 import jax.numpy as jnp
 from jax import lax
 from jax.sharding import PartitionSpec as P
+
+
+def supply_all_chunk(vector):
+    mid_arr = lax.axis_index("row")
+    met_up = lax.axis_size("row")
+    extra, frame_out, block_next = (met_up, mid_arr, vector.shape[0])
+    bank = [(p, (p + 1) % extra) for p in range(extra)]
+    wide_out = jnp.zeros((*vector.shape[:0], extra * block_next, *vector.shape[1:]), vector.dtype)
+    table = [(p, (p - 1) % extra) for p in range(extra)]
+    wide_out = lax.dynamic_update_slice_in_dim(wide_out, vector, frame_out * block_next, axis=0)
+    block_last = extra // 2
+    all_values = long_array = vector
+    for ix in range(1, block_last + 1):
+        all_values = lax.ppermute(all_values, "row", bank)
+        wide_out = lax.dynamic_update_slice_in_dim(
+            wide_out, all_values, (frame_out - ix) % extra * block_next, axis=0
+        )
+        if ix < extra - block_last:
+            long_array = lax.ppermute(long_array, "row", table)
+            wide_out = lax.dynamic_update_slice_in_dim(
+                wide_out, long_array, (frame_out + ix) % extra * block_next, axis=0
+            )
+    return wide_out
 
 
 def mask_left(block_tile, pattern):
@@ -32,9 +55,7 @@
     layers = lax.axis_size("layer")
     column_span = right_tile.shape[1] // layers
     partial_value = jnp.dot(
-        whole_left,
-        lax.all_gather(right_tile, "row", axis=0, tiled=True),
-        preferred_element_type=jnp.float32,
+        whole_left, supply_all_chunk(right_tile), preferred_element_type=jnp.float32
     )
     return lax.psum_scatter(
         partial_value.reshape(row_count, layers, column_span),

time: 162 us -> 112 us (0.69)
  waiting for transfers between devices: 130 us -> 72.6 us
  starting transfers between devices: 0.21 us -> 9.18 us
    all_gather x2 -> x0, waiting for transfers between devices: 56.5 us -> none  [multiply(): lax.all_gather(right_tile, 'row', axis=0, tiled=True)]
    all_gather x2, waiting for transfers between devices: 35.6 us -> 0.04 us  [multiply(): whole_left = lax.all_gather(left_tile, 'col', axis=1, tiled=True)]
    ppermute x0 -> x6, waiting for transfers between devices: none -> 34.7 us  [the longest x4 26.1 us: supply_all_chunk(): all_values = lax.ppermute(all_values, 'row', bank)]
    ppermute x0 -> x6, starting transfers between devices: none -> 9.05 us  [the longest x4 4.62 us: supply_all_chunk(): all_values = lax.ppermute(all_values, 'row', bank)]
  transfers between devices with their start and end apart: 6 -> 10, of which waited for: 6 -> 8; matrix products, arithmetic and copies ran while one was open for 3% -> 1% of each run, Pallas kernels for 0% -> 0%
where the time goes in v1:
time: 112 us
  waiting for transfers between devices  72.6 us (65%)
  between operations  13.3 us (12%)
  starting transfers between devices  9.18 us (8%)
  local copies, waits for them, and re-layouts  6.39 us (6%)
  other arithmetic  5.22 us (5%)
  matrix products  4.95 us (4%)
    reduce_scatter x2, waiting for transfers between devices, multiply(): lax.psum_scatter(partial_value.reshape(row_count, layers, column_span), '...  37.8 us
    ppermute x4, waiting for transfers between devices, supply_all_chunk(): all_values = lax.ppermute(all_values, 'row', bank)  26.1 us
    ppermute x2, waiting for transfers between devices, supply_all_chunk(): long_array = lax.ppermute(long_array, 'row', table)  8.64 us
    dot_general x2, matrix products, multiply(): jnp.dot(whole_left, supply_all_chunk(right_tile), preferred_element_type=...  4.95 us
    ppermute x4, starting transfers between devices, supply_all_chunk(): all_values = lax.ppermute(all_values, 'row', bank)  4.62 us
    ppermute x2, starting transfers between devices, supply_all_chunk(): long_array = lax.ppermute(long_array, 'row', table)  4.43 us
    unnamed x14, local copies, waits for them, and re-layouts  3.71 us
    mul x2, other arithmetic, mask_left(): blocks * pattern.reshape(row_blocks, 1, col_blocks, 1).astype(jnp.bfloat16)  2.55 us
  transfers between devices with their start and end apart: 10, of which 8 were waited for; matrix products, arithmetic and copies ran while one was open for 1% of the time, Pallas kernels for 0%

profile of v1, /device:TPU:0, one launch (start us, length us, event | category | flops | bytes accessed | tf_op | source)
XLA Modules:
  0.0 111.6 jit_solution(12681633929771606329)
XLA Ops:
  6.5 0.0 copy-start
  6.5 0.0 all-gather.3.cloned.1.call-start
  6.5 0.7 convert_bitcast_fusion.3
  7.3 0.1 copy.8
  7.4 0.2 mul.60
  7.6 0.0 copy-done
  7.6 0.7 bitcast_multiply_fusion.1
  8.3 0.0 copy-start.1
  8.3 0.0 all-gather.3.cloned.1.call-update
  8.4 0.0 reduce-scatter.3.cloned.1.call-start
  8.4 0.9 copy-done.1
  9.3 0.0 copy-start.3
  9.3 0.6 copy-done.3
  10.0 0.2 mul.63
  10.2 0.1 mul.64
  10.3 0.1 broadcast.10.clone
  10.4 0.1 constant_dynamic-update-slice_fusion.7
  10.5 3.1 %collective-permute-start = (bf16[256,512]{1,0:T(8,128)(2,1)S(1)}, bf16[256,512]{1,0:T(8,128)(2,1)S(1)}, u32[]{:S(2)}, u32[]{:S(2)}) collective-permute-start(bf16[256,512]{1,0:T(8,128)(2,1)S(1)} %get-tuple-element.8), channel_id=1, source_target_pairs={{0,8},{8,16},{16,24},{24,0},{1,9},{9,17},{17,25},{25,1},{2,10},{10... | collective-permute-start | bytes 786440 | tf_op jit(solution)/shard_map/ppermute | solution.py:18
  13.5 2.1 %collective-permute-start.1 = (bf16[256,512]{1,0:T(8,128)(2,1)S(1)}, bf16[256,512]{1,0:T(8,128)(2,1)S(1)}, u32[]{:S(2)}, u32[]{:S(2)}) collective-permute-start(bf16[256,512]{1,0:T(8,128)(2,1)S(1)} %get-tuple-element.8), channel_id=1, source_target_pairs={{0,24},{8,0},{16,8},{24,16},{1,25},{9,1},{17,9},{25,17},{2,26},{10... | collective-permute-start | bytes 786440 | tf_op jit(solution)/shard_map/ppermute | solution.py:23
  15.6 7.1 %collective-permute-done = bf16[256,512]{1,0:T(8,128)(2,1)S(1)} collective-permute-done((bf16[256,512]{1,0:T(8,128)(2,1)S(1)}, bf16[256,512]{1,0:T(8,128)(2,1)S(1)}, u32[]{:S(2)}, u32[]{:S(2)}) %collective-permute-start) | collective-permute-done | bytes 262176 | tf_op jit(solution)/shard_map/ppermute | solution.py:18
  22.7 0.0 collective-permute-start.2
  22.8 4.4 %collective-permute-done.1 = bf16[256,512]{1,0:T(8,128)(2,1)S(1)} collective-permute-done((bf16[256,512]{1,0:T(8,128)(2,1)S(1)}, bf16[256,512]{1,0:T(8,128)(2,1)S(1)}, u32[]{:S(2)}, u32[]{:S(2)}) %collective-permute-start.1) | collective-permute-done | bytes 262176 | tf_op jit(solution)/shard_map/ppermute | solution.py:23
  27.2 6.0 %collective-permute-done.2 = bf16[256,512]{1,0:T(8,128)(2,1)S(1)} collective-permute-done((bf16[256,512]{1,0:T(8,128)(2,1)S(1)}, bf16[256,512]{1,0:T(8,128)(2,1)S(1)}, u32[]{:S(2)}, u32[]{:S(2)}) %collective-permute-start.2) | collective-permute-done | bytes 262176 | tf_op jit(solution)/shard_map/ppermute | solution.py:18
  33.2 0.0 all-gather.3.cloned.1.call-done
  33.2 3.0 %fusion = f32[512,512]{0,1:T(8,128)} fusion(bf16[512,1024]{1,0:T(8,128)(2,1)} %all-gather.3.cloned.1.call-done, bf16[1024,512]{1,0:T(8,128)(2,1)S(1)} %constant_dynamic-update-slice_fusion.4), kind=kOutput, calls=%fused_computation.14 | convolution fusion | flops 536870912 | bytes 3145728 | tf_op jit(solution)/shard_map/dot_general | solution.py:57
  36.2 0.0 copy-start.5
  36.2 0.0 reduce-scatter.3.cloned.1.call-update
  36.2 0.0 all-gather.5.cloned.1.call-start
  36.3 0.6 copy-done.5
  36.9 19.1 %reduce-scatter.3.cloned.1.call-done = f32[512,1,256]{0,2,1:T(8,128)} async-done(((f32[512,2,256]{0,2,1:T(8,128)}), f32[512,1,256]{0,2,1:T(8,128)}) %reduce-scatter.3.cloned.1.call-update) | async-done | bytes 524304 | tf_op jit(solution)/shard_map/reduce_scatter | solution.py:60
  56.0 0.1 mul.70
  56.2 1.8 %bitcast_multiply_fusion = bf16[512,256]{0,1:T(8,128)(2,1)} fusion(bf16[32,8,4,128]{3,2,1,0:T(4,128)(2,1)S(1)} %bitcast.39, f32[512,1,256]{0,2,1:T(8,128)} %reduce-scatter.3.cloned.1.call-done), kind=kLoop, calls=%fused_computation | loop fusion | flops 262144 | bytes 1048576 | tf_op jit(solution)/shard_map/mul | solution.py:37
  58.0 0.0 copy-start.2
  58.0 0.0 all-gather.5.cloned.1.call-update
  58.0 0.0 reduce-scatter.5.cloned.1.call-start
  58.0 0.9 copy-done.2
  58.9 0.0 copy-start.4
  58.9 0.6 copy-done.4
  59.6 0.2 mul.73
  59.8 0.1 mul.74
  59.9 0.1 broadcast.10.clone.1
  60.0 0.1 constant_dynamic-update-slice_fusion.3
  60.1 1.5 %collective-permute-start.3 = (bf16[256,512]{1,0:T(8,128)(2,1)S(1)}, bf16[256,512]{1,0:T(8,128)(2,1)S(1)}, u32[]{:S(2)}, u32[]{:S(2)}) collective-permute-start(bf16[256,512]{1,0:T(8,128)(2,1)S(1)} %get-tuple-element.6), channel_id=1, source_target_pairs={{0,8},{8,16},{16,24},{24,0},{1,9},{9,17},{17,25},{25,1},{2,10},{10... | collective-permute-start | bytes 786440 | tf_op jit(solution)/shard_map/ppermute | solution.py:18
  61.6 2.3 %collective-permute-start.4 = (bf16[256,512]{1,0:T(8,128)(2,1)S(1)}, bf16[256,512]{1,0:T(8,128)(2,1)S(1)}, u32[]{:S(2)}, u32[]{:S(2)}) collective-permute-start(bf16[256,512]{1,0:T(8,128)(2,1)S(1)} %get-tuple-element.6), channel_id=1, source_target_pairs={{0,24},{8,0},{16,8},{24,16},{1,25},{9,1},{17,9},{25,17},{2,26},{10... | collective-permute-start | bytes 786440 | tf_op jit(solution)/shard_map/ppermute | solution.py:23
  64.0 7.2 %collective-permute-done.3 = bf16[256,512]{1,0:T(8,128)(2,1)S(1)} collective-permute-done((bf16[256,512]{1,0:T(8,128)(2,1)S(1)}, bf16[256,512]{1,0:T(8,128)(2,1)S(1)}, u32[]{:S(2)}, u32[]{:S(2)}) %collective-permute-start.3) | collective-permute-done | bytes 262176 | tf_op jit(solution)/shard_map/ppermute | solution.py:18
  71.2 0.0 collective-permute-start.5
  71.2 4.3 %collective-permute-done.4 = bf16[256,512]{1,0:T(8,128)(2,1)S(1)} collective-permute-done((bf16[256,512]{1,0:T(8,128)(2,1)S(1)}, bf16[256,512]{1,0:T(8,128)(2,1)S(1)}, u32[]{:S(2)}, u32[]{:S(2)}) %collective-permute-start.4) | collective-permute-done | bytes 262176 | tf_op jit(solution)/shard_map/ppermute | solution.py:23
  75.5 5.8 %collective-permute-done.5 = bf16[256,512]{1,0:T(8,128)(2,1)S(1)} collective-permute-done((bf16[256,512]{1,0:T(8,128)(2,1)S(1)}, bf16[256,512]{1,0:T(8,128)(2,1)S(1)}, u32[]{:S(2)}, u32[]{:S(2)}) %collective-permute-start.5) | collective-permute-done | bytes 262176 | tf_op jit(solution)/shard_map/ppermute | solution.py:18
  81.3 0.0 all-gather.5.cloned.1.call-done
  81.3 2.0 %fusion.1 = f32[512,512]{0,1:T(8,128)S(1)} fusion(bf16[512,1024]{0,1:T(8,128)(2,1)} %all-gather.5.cloned.1.call-done, bf16[1024,512]{1,0:T(8,128)(2,1)S(1)} %constant_dynamic-update-slice_fusion), kind=kOutput, calls=%fused_computation.15 | convolution fusion | flops 536870912 | bytes 3145728 | tf_op jit(solution)/shard_map/dot_general | solution.py:57
  83.3 1.3 %copy.9 = f32[512,2,256]{2,0,1:T(8,128)} copy(f32[512,2,256]{0,2,1:T(8,128)S(1)} %bitcast.36) | data formatting | bytes 2097152 | tf_op jit(solution)/shard_map/reshape | solution.py:61
  84.6 0.0 reduce-scatter.5.cloned.1.call-update
  84.7 18.6 %reduce-scatter.5.cloned.1.call-done = f32[512,1,256]{2,0,1:T(8,128)} async-done(((f32[512,2,256]{2,0,1:T(8,128)}), f32[512,1,256]{2,0,1:T(8,128)}) %reduce-scatter.5.cloned.1.call-update) | async-done | bytes 524304 | tf_op jit(solution)/shard_map/reduce_scatter | solution.py:60
  103.3 1.8 %convert_element_type.59 = bf16[512,1,256]{2,0,1:T(8,128)(2,1)} convert(f32[512,1,256]{2,0,1:T(8,128)} %reduce-scatter.5.cloned.1.call-done) | non-fusion elementwise | flops 131072 | bytes 786432 | tf_op jit(solution)/shard_map/convert_element_type | solution.py:82
  (11 shorter events, 0.2 us)
Async XLA Ops:
  6.5 1.1 copy-start
  6.5 26.7 %all-gather.3.cloned.1.call-start = ((), (), s32[]{:S(2)}) async-start(), calls=%async_computation.2 | async-start | bytes 1310720 | tf_op jit(solution)/shard_map/all_gather | solution.py:53
  8.3 0.9 copy-start.1
  8.4 47.6 %reduce-scatter.3.cloned.1.call-start = ((), (), s32[]{:S(2)}) async-start(), calls=%async_computation.3 | async-start | bytes 1572864 | tf_op jit(solution)/shard_map/reduce_scatter | solution.py:60
  9.3 0.7 copy-start.3
  10.5 12.3 %collective-permute-start = (bf16[256,512]{1,0:T(8,128)(2,1)S(1)}, bf16[256,512]{1,0:T(8,128)(2,1)S(1)}, u32[]{:S(2)}, u32[]{:S(2)}) collective-permute-start(bf16[256,512]{1,0:T(8,128)(2,1)S(1)} %get-tuple-element.8), channel_id=1, source_target_pairs={{0,8},{8,16},{16,24},{24,0},{1,9},{9,17},{17,25},{25,1},{2,10},{10... | collective-permute-start | bytes 786440 | tf_op jit(solution)/shard_map/ppermute | solution.py:18
  13.5 13.6 %collective-permute-start.1 = (bf16[256,512]{1,0:T(8,128)(2,1)S(1)}, bf16[256,512]{1,0:T(8,128)(2,1)S(1)}, u32[]{:S(2)}, u32[]{:S(2)}) collective-permute-start(bf16[256,512]{1,0:T(8,128)(2,1)S(1)} %get-tuple-element.8), channel_id=1, source_target_pairs={{0,24},{8,0},{16,8},{24,16},{1,25},{9,1},{17,9},{25,17},{2,26},{10... | collective-permute-start | bytes 786440 | tf_op jit(solution)/shard_map/ppermute | solution.py:23
  22.7 10.4 %collective-permute-start.2 = (bf16[256,512]{1,0:T(8,128)(2,1)S(1)}, bf16[256,512]{1,0:T(8,128)(2,1)S(1)}, u32[]{:S(2)}, u32[]{:S(2)}) collective-permute-start(bf16[256,512]{1,0:T(8,128)(2,1)S(1)} %collective-permute-done), channel_id=1, source_target_pairs={{0,8},{8,16},{16,24},{24,0},{1,9},{9,17},{17,25},{25,1},{2,10},{10... | collective-permute-start | bytes 786440 | tf_op jit(solution)/shard_map/ppermute | solution.py:18
  36.2 0.7 copy-start.5
  36.2 45.1 %all-gather.5.cloned.1.call-start = ((), (), s32[]{:S(2)}) async-start(), calls=%async_computation.4 | async-start | bytes 1310720 | tf_op jit(solution)/shard_map/all_gather | solution.py:53
  58.0 0.9 copy-start.2
  58.0 45.3 %reduce-scatter.5.cloned.1.call-start = ((), (), s32[]{:S(2)}) async-start(), calls=%async_computation.5 | async-start | bytes 1572864 | tf_op jit(solution)/shard_map/reduce_scatter | solution.py:60
  58.9 0.7 copy-start.4
  60.1 11.1 %collective-permute-start.3 = (bf16[256,512]{1,0:T(8,128)(2,1)S(1)}, bf16[256,512]{1,0:T(8,128)(2,1)S(1)}, u32[]{:S(2)}, u32[]{:S(2)}) collective-permute-start(bf16[256,512]{1,0:T(8,128)(2,1)S(1)} %get-tuple-element.6), channel_id=1, source_target_pairs={{0,8},{8,16},{16,24},{24,0},{1,9},{9,17},{17,25},{25,1},{2,10},{10... | collective-permute-start | bytes 786440 | tf_op jit(solution)/shard_map/ppermute | solution.py:18
  61.6 13.9 %collective-permute-start.4 = (bf16[256,512]{1,0:T(8,128)(2,1)S(1)}, bf16[256,512]{1,0:T(8,128)(2,1)S(1)}, u32[]{:S(2)}, u32[]{:S(2)}) collective-permute-start(bf16[256,512]{1,0:T(8,128)(2,1)S(1)} %get-tuple-element.6), channel_id=1, source_target_pairs={{0,24},{8,0},{16,8},{24,16},{1,25},{9,1},{17,9},{25,17},{2,26},{10... | collective-permute-start | bytes 786440 | tf_op jit(solution)/shard_map/ppermute | solution.py:23
  71.2 10.1 %collective-permute-start.5 = (bf16[256,512]{1,0:T(8,128)(2,1)S(1)}, bf16[256,512]{1,0:T(8,128)(2,1)S(1)}, u32[]{:S(2)}, u32[]{:S(2)}) collective-permute-start(bf16[256,512]{1,0:T(8,128)(2,1)S(1)} %collective-permute-done.3), channel_id=1, source_target_pairs={{0,8},{8,16},{16,24},{24,0},{1,9},{9,17},{17,25},{25,1},{2,10},{10... | collective-permute-start | bytes 786440 | tf_op jit(solution)/shard_map/ppermute | solution.py:18
Sparse Core Ops, SparseCore 0:
  8.9 19.5 all-gather.2
  36.3 19.6 reduce-scatter.2
  58.1 16.7 all-gather.4
  84.8 18.4 reduce-scatter.4
